TPU v7x, 512 devices: a whole 4x4x16 slice. The times are simulated.
512 devices in a mesh: lon: 32 (over z_lo, x), ch: 16 (over z_hi, y, core).
Axes of the slice: x: 4, y: 4, z: 16 (z_hi: 2, z_lo: 8; z = z_hi * 8 + z_lo), core: 2. Of those that a mesh axis runs over, the one named last changes fastest.
Arguments:
- inputs: bfloat16 [1, 4, 48, 64, 512], P(None, None, None, 'lon', 'ch'), may hold values from -6 to 6
- grad_out: bfloat16 [1, 4, 48, 64, 512], P(None, None, None, 'lon', 'ch'), may hold values from -6 to 6
- kernel: bfloat16 [3, 3, 3, 512, 512], P(None, None, None, 'ch'), may hold values from -0.0546875 to 0.0546875
Outputs:
- grad_in: bfloat16 [1, 4, 48, 64, 512], P(None, None, None, 'lon', 'ch')
- grad_kernel: float32 [3, 3, 3, 512, 512], P(None, None, None, 'ch', 'lon')
All inputs are finite; a program needn't handle non-finite values.
Results may differ from a plain program's by a relative error of at most 0.0012.
Values may be sent and summed in bfloat16 or wider, within the bound.
A program may use at most 64 MiB of HBM per device.

v0:
```python
import math
import jax
import jax.numpy as jnp
from jax import lax
from jax.sharding import PartitionSpec as P


def with_halo(cells, sides, width):
    for axis, dim in sides:
        count = lax.axis_size(axis)
        head = lax.slice_in_dim(cells, 0, width, axis=dim)
        tail = lax.slice_in_dim(cells, cells.shape[dim] - width, cells.shape[dim], axis=dim)
        cells = jnp.concatenate(
            [
                lax.ppermute(tail, axis, [(i, (i + 1) % count) for i in range(count)]),
                cells,
                lax.ppermute(head, axis, [((i + 1) % count, i) for i in range(count)]),
            ],
            axis=dim,
        )
    return cells


def contract_rows(left, right):
    return lax.dot_general(
        left, right, (((0,), (0,)), ((), ())), preferred_element_type=jnp.float32
    )


def tap_product(grad_all, kernel, step_t):
    out_width = grad_all.shape[4]
    cin_loc = kernel.shape[3]
    stacked = kernel[step_t].transpose(3, 0, 1, 2).reshape(out_width, 9 * cin_loc)
    product = jnp.dot(grad_all.reshape(-1, out_width), stacked, preferred_element_type=jnp.float32)
    return product.reshape(grad_all.shape[:4] + (3, 3, cin_loc))


def body(inputs, grad_out, kernel):
    batches, frames, lat_cells, lon_cols, cin_loc = inputs.shape
    lon_cells = lon_cols * lax.axis_size("lon")
    rscale = 1.0 / math.sqrt(batches * frames * lat_cells * lon_cells)
    grad_ext = with_halo(grad_out, (("lon", 3),), 1)
    grad_all = lax.all_gather(grad_ext, "ch", axis=4, tiled=True)
    out_width = grad_all.shape[4]
    accum_dx = jnp.zeros((batches, frames, lat_cells, lon_cols, cin_loc), jnp.float32)
    for step_t in range(3):
        product = tap_product(grad_all, kernel, step_t)
        padded = jnp.pad(product, ((0, 0), (1, 1), (1, 1), (0, 0), (0, 0), (0, 0), (0, 0)))
        for step_h in range(3):
            for step_w in range(3):
                accum_dx = (
                    accum_dx
                    + padded[
                        :,
                        2 - step_t : 2 - step_t + frames,
                        2 - step_h : 2 - step_h + lat_cells,
                        2 - step_w : 2 - step_w + lon_cols,
                        step_h,
                        step_w,
                        :,
                    ]
                )
    grad_in = accum_dx.astype(jnp.bfloat16)
    tap_terms = []
    shifted = jnp.stack(
        [
            jnp.pad(inputs, ((0, 0), (0, 0), (0, 0), (2 - step_w, step_w), (0, 0)))
            for step_w in range(3)
        ],
        axis=4,
    )
    x_pad = jnp.pad(shifted, ((0, 0), (1, 1), (1, 1), (0, 0), (0, 0), (0, 0)))
    flat_grad = grad_all.reshape(-1, out_width)
    for step_t in range(3):
        x_block = jnp.stack(
            [
                x_pad[:, step_t : step_t + frames, step_h : step_h + lat_cells]
                for step_h in range(3)
            ],
            axis=4,
        )
        tap_terms.append(
            contract_rows(x_block.reshape(-1, 9 * cin_loc), flat_grad).reshape(
                3, 3, cin_loc, out_width
            )
        )
    weight_terms = jnp.stack(tap_terms) * rscale
    grad_kernel = lax.psum_scatter(weight_terms, "lon", scatter_dimension=4, tiled=True)
    return (grad_in, grad_kernel)


def solution(mesh):
    return jax.shard_map(
        body,
        mesh=mesh,
        in_specs=(
            P(None, None, None, "lon", "ch"),
            P(None, None, None, "lon", "ch"),
            P(None, None, None, "ch", None),
        ),
        out_specs=(P(None, None, None, "lon", "ch"), P(None, None, None, "ch", "lon")),
        check_vma=False,
    )
```

profile of v0, /device:TPU:8, one launch (start us, length us, event | category | flops | bytes accessed | tf_op | source)
XLA Modules:
  0.0 632.7 jit_solution(9007344255820453416)
XLA Ops:
  7.2 0.0 all-reduce.10.cloned.1.call-start
  7.2 0.9 copy.40
  8.1 0.0 copy-start.5
  8.1 0.6 copy-done.5
  8.7 0.7 fusion.63
  9.5 15.3 %collective-permute-start.1 = (bf16[1,4,48,1,32]{2,3,1,0,4:T(2,128)(2,1)}, bf16[1,4,48,1,32]{2,3,1,0,4:T(2,128)(2,1)}, u32[]{:S(2)}, u32[]{:S(2)}) collective-permute-start(bf16[1,4,48,1,32]{2,3,1,0,4:T(2,128)(2,1)} %get-tuple-element.22), channel_id=1, source_target_pairs={{16,0},{32,16},{48,32},{64,48},{80,64},{96,80},{112,96},{128,112},... | collective-permute-start | bytes 36872 | tf_op jit(solution)/shard_map/ppermute | solution.py:17
  24.8 1.9 collective-permute-start
  26.7 1.0 pad_bitcast_fusion.2
  27.8 0.1 fusion.62
  27.9 0.8 fusion.6
  28.7 2.0 pad_maximum_fusion
  30.7 0.3 pad_maximum_fusion.2
  31.0 2.1 copy.59
  33.1 0.0 copy-start.1
  33.1 2.3 reshape.403
  35.4 2.0 copy.60
  37.4 0.0 copy-done.1
  37.4 2.1 copy.57
  39.5 2.3 reshape.401
  41.8 2.1 copy.58
  43.8 2.1 copy.54
  45.9 0.0 copy-start.6
  45.9 1.3 reshape.398
  47.2 1.0 copy.55
  48.2 0.0 collective-permute-done.1
  48.2 0.0 collective-permute-done
  48.2 1.1 pad_maximum_fusion.4
  49.4 49.3 %all_gather.3 = bf16[1,4,48,4,512]{2,3,1,0,4:T(4,128)(2,1)S(1)} all-gather(bf16[1,4,48,4,32]{2,3,1,0,4:T(4,128)(2,1)S(1)} %pad_maximum_fusion.4), channel_id=1, replica_groups=mesh['lon'=32,'ch'=16] {'ch'}, dimensions={4}, use_global_device_ids=true | all-gather | bytes 835584 | tf_op jit(solution)/shard_map/all_gather | solution.py:43
  98.7 2.9 copy.56
  101.5 1.6 reshape.421
  103.1 0.4 convolution_bitcast_fusion.3
  103.5 0.6 copy-done.3
  104.1 0.4 convolution_bitcast_fusion.4
  104.5 0.0 copy-done.4
  104.5 0.4 convolution_bitcast_fusion.5
  104.9 1.4 maximum_multiply_fusion
  106.3 8.7 %copy.61 = f32[3,3,3,32,512]{3,2,1,0,4:T(4,128)} copy(f32[3,3,3,32,512]{4,3,2,1,0:T(8,128)} %maximum_multiply_fusion) | data formatting | bytes 3538944 | tf_op jit(solution)/shard_map/mul | solution.py:87
  115.0 0.0 all-reduce.10.cloned.1.call-update
  115.0 1.3 dynamic-slice
  116.9 1.8 copy.43
  118.8 0.0 copy-start.7
  118.8 1.8 convolution_bitcast_fusion
  120.6 0.8 convolution_bitcast_fusion.1
  121.4 0.8 convolution_bitcast_fusion.2
  122.2 1.2 fusion.61
  123.4 500.7 %all-reduce.10.cloned.1.call-done = f32[3,3,3,32,512]{3,2,1,0,4:T(4,128)} async-done(((f32[3,3,3,32,512]{3,2,1,0,4:T(4,128)}), f32[3,3,3,32,512]{3,2,1,0,4:T(4,128)}) %all-reduce.10.cloned.1.call-update) | async-done | bytes 1769488
  624.1 1.0 constant_dynamic-slice_fusion
  625.1 0.7 copy.62
  (8 shorter events, 0.0 us)
Async XLA Ops:
  7.2 617.0 %all-reduce.10.cloned.1.call-start = ((), (), s32[]{:S(2)}) async-start(), calls=%async_computation | async-start | bytes 18874368
  8.1 0.6 copy-start.5
  9.5 38.8 %collective-permute-start.1 = (bf16[1,4,48,1,32]{2,3,1,0,4:T(2,128)(2,1)}, bf16[1,4,48,1,32]{2,3,1,0,4:T(2,128)(2,1)}, u32[]{:S(2)}, u32[]{:S(2)}) collective-permute-start(bf16[1,4,48,1,32]{2,3,1,0,4:T(2,128)(2,1)} %get-tuple-element.22), channel_id=1, source_target_pairs={{16,0},{32,16},{48,32},{64,48},{80,64},{96,80},{112,96},{128,112},... | collective-permute-start | bytes 36872 | tf_op jit(solution)/shard_map/ppermute | solution.py:17
  24.8 23.4 %collective-permute-start = (bf16[1,4,48,1,32]{2,3,1,0,4:T(2,128)(2,1)}, bf16[1,4,48,1,32]{2,3,1,0,4:T(2,128)(2,1)}, u32[]{:S(2)}, u32[]{:S(2)}) collective-permute-start(bf16[1,4,48,1,32]{2,3,1,0,4:T(2,128)(2,1)} %get-tuple-element.21), channel_id=1, source_target_pairs={{0,16},{16,32},{32,48},{48,64},{64,80},{80,96},{96,112},{112,128},... | collective-permute-start | bytes 36872 | tf_op jit(solution)/shard_map/ppermute | solution.py:15
  33.1 4.3 copy-start.1
  39.5 4.4 copy-start
  45.9 2.3 copy-start.6
  98.7 4.4 copy-start.2
  103.1 1.0 copy-start.3
  103.1 1.4 copy-start.4
  118.8 1.8 copy-start.7
Sparse Core Ops, SparseCore 0:
  115.1 508.9 all-reduce.9
where the time goes:
time: 633 us
  waiting for transfers between devices  501 us (79%)
  blocking collectives  49.3 us (8%)
  local copies, waits for them, and re-layouts  39.7 us (6%)
  starting transfers between devices  17.3 us (3%)
  between operations  14.9 us (2%)
    unnamed x2, waiting for transfers between devices  501 us
    all_gather x1, blocking collectives, body(): grad_all = lax.all_gather(grad_ext, 'ch', axis=4, tiled=True)  49.3 us
    ppermute x1, starting transfers between devices, with_halo(): lax.ppermute(head, axis, [((i + 1) % count, i) for i in range(count)])  15.3 us
  transfers between devices with their start and end apart: 3, of which 1 were waited for; matrix products, arithmetic and copies ran while one was open for 5% of the time, Pallas kernels for 0%

commit v1 on v0

--- a/solution.py
+++ b/solution.py
@@ -40,7 +40,10 @@
     lon_cells = lon_cols * lax.axis_size("lon")
     rscale = 1.0 / math.sqrt(batches * frames * lat_cells * lon_cells)
     grad_ext = with_halo(grad_out, (("lon", 3),), 1)
-    grad_all = lax.all_gather(grad_ext, "ch", axis=4, tiled=True)
+    size = lax.axis_size("ch")
+    pieces = jnp.stack([grad_ext for _ in range(size)])
+    pieces = lax.all_to_all(pieces, "ch", split_axis=0, concat_axis=0)
+    grad_all = jnp.concatenate(pieces, axis=4)
     out_width = grad_all.shape[4]
     accum_dx = jnp.zeros((batches, frames, lat_cells, lon_cols, cin_loc), jnp.float32)
     for step_t in range(3):

time: 633 us -> 613 us (0.968)
  blocking collectives: 49.3 us -> 0 us
  local copies, waits for them, and re-layouts: 39.7 us -> 67.7 us
  starting transfers between devices: 17.3 us -> 28.2 us
  waiting for transfers between devices: 501 us -> 491 us
    all_gather x1 -> x0, blocking collectives: 49.3 us -> none  [body(): grad_all = lax.all_gather(grad_ext, 'ch', axis=4, tiled=True)]
    unnamed x2, waiting for transfers between devices: 501 us -> 477 us
    ppermute x1, waiting for transfers between devices: 0.01 us -> 12.6 us  [with_halo(): lax.ppermute(tail, axis, [(i, (i + 1) % count) for i in range(count)])]
    all_to_all x0 -> x1, starting transfers between devices: none -> 10.7 us  [body(): pieces = lax.all_to_all(pieces, 'ch', split_axis=0, concat_axis=0)]
    reshape x1 -> x3, local copies, waits for them, and re-layouts: 1.56 us -> 11.4 us  [body(): grad_all = jnp.concatenate(pieces, axis=4)]
    another operation x0 -> x2, local copies, waits for them, and re-layouts: none -> 9.3 us
    reshape x3, local copies, waits for them, and re-layouts: 5.82 us -> 12.4 us  [body(): x_block.reshape(-1, 9 * cin_loc)]
  transfers between devices with their start and end apart: 3 -> 4, of which waited for: 1 -> 3; matrix products, arithmetic and copies ran while one was open for 5% -> 7% of each run, Pallas kernels for 0% -> 0%
where the time goes in v1:
time: 613 us; the launch traced here: 612 us
  waiting for transfers between devices  491 us (80%)
  local copies, waits for them, and re-layouts  67.7 us (11%)
  starting transfers between devices  28.2 us (5%)
  between operations  14.9 us (2%)
  other arithmetic  6.84 us (1%)
    unnamed x2, waiting for transfers between devices  477 us
    ppermute x1, starting transfers between devices, with_halo(): lax.ppermute(head, axis, [((i + 1) % count, i) for i in range(count)])  15.3 us
    ppermute x1, waiting for transfers between devices, with_halo(): lax.ppermute(tail, axis, [(i, (i + 1) % count) for i in range(count)])  12.6 us
    reshape x3, local copies, waits for them, and re-layouts, body(): x_block.reshape(-1, 9 * cin_loc)  12.4 us
  transfers between devices with their start and end apart: 4, of which 3 were waited for; matrix products, arithmetic and copies ran while one was open for 7% of the time, Pallas kernels for 0%

profile of v1, /device:TPU:8, one launch (start us, length us, event | category | flops | bytes accessed | tf_op | source)
XLA Modules:
  0.0 612.4 jit_solution(14923154501753116178)
XLA Ops:
  7.2 0.8 fusion.63
  8.0 15.3 %collective-permute-start.1 = (bf16[1,4,48,1,32]{2,4,3,1,0:T(8,128)(2,1)S(1)}, bf16[1,4,48,1,32]{2,4,3,1,0:T(8,128)(2,1)S(1)}, u32[]{:S(2)}, u32[]{:S(2)}) collective-permute-start(bf16[1,4,48,1,32]{2,4,3,1,0:T(8,128)(2,1)S(1)} %get-tuple-element.22), channel_id=1, source_target_pairs={{16,0},{32,16},{48,32},{64,48},{80,64},{96,80},{112,96},{128,112},... | collective-permute-start | bytes 36872 | tf_op jit(solution)/shard_map/ppermute | solution.py:17
  23.3 1.9 collective-permute-start
  25.2 0.0 collective-permute-done.1
  25.2 12.6 %collective-permute-done = bf16[1,4,48,1,32]{2,4,3,1,0:T(8,128)(2,1)S(1)} collective-permute-done((bf16[1,4,48,1,32]{2,4,3,1,0:T(8,128)(2,1)S(1)}, bf16[1,4,48,1,32]{2,4,3,1,0:T(8,128)(2,1)S(1)}, u32[]{:S(2)}, u32[]{:S(2)}) %collective-permute-start) | collective-permute-done | bytes 12320 | tf_op jit(solution)/shard_map/ppermute | solution.py:15
  37.8 0.9 maximum_bitcast_fusion
  38.7 0.5 broadcast_bitcast_fusion
  39.2 0.0 copy-start.4
  39.2 3.9 reshape.428
  43.1 10.7 %all-to-all-start = ((bf16[16,2,12288]{2,1,0:T(2,128)(2,1)}), bf16[16,2,12288]{2,1,0:T(2,128)(2,1)S(1)}, u32[]{:S(2)}, u32[]{:S(2)}) async-start(bf16[16,2,12288]{2,1,0:T(2,128)(2,1)} %reshape.428), calls=%async_computation | async-start | bytes 1572864 | tf_op jit(solution)/shard_map/all_to_all | solution.py:45
  53.7 0.2 all-reduce.10.cloned.1.call-start
  54.0 0.1 pad_bitcast_fusion.2
  54.0 0.9 fusion.62
  54.9 1.9 fusion.6
  56.8 0.3 pad_maximum_fusion.2
  57.1 3.1 copy.53
  60.2 4.1 reshape.406
  64.3 1.0 copy.54
  65.3 2.2 pad_maximum_fusion
  67.5 3.1 copy.51
  70.6 4.1 reshape.404
  74.7 1.0 copy.52
  75.7 3.1 copy.48
  78.8 4.1 reshape.402
  82.9 1.0 copy.49
  83.9 1.2 all-to-all-done
  85.1 3.1 reshape.429
  88.1 2.2 bitcast_bitcast_fusion
  90.4 5.5 copy.50
  95.9 4.6 reshape.424
  100.5 0.4 convolution_bitcast_fusion.3
  100.9 0.6 copy-done.1
  101.5 0.4 convolution_bitcast_fusion.4
  101.9 0.0 copy-done.2
  101.9 0.4 convolution_bitcast_fusion.5
  102.3 1.4 maximum_multiply_fusion
  103.8 8.7 %copy.55 = f32[3,3,3,32,512]{3,2,1,0,4:T(4,128)} copy(f32[3,3,3,32,512]{4,3,2,1,0:T(8,128)} %maximum_multiply_fusion) | data formatting | bytes 3538944 | tf_op jit(solution)/shard_map/mul | solution.py:90
  112.5 0.0 all-reduce.10.cloned.1.call-update
  112.5 1.3 dynamic-slice
  114.4 3.7 copy.37
  118.1 4.7 reshape.420
  122.7 0.8 convolution_bitcast_fusion
  123.5 0.8 convolution_bitcast_fusion.1
  124.3 0.8 convolution_bitcast_fusion.2
  125.1 1.2 fusion.61
  126.3 477.5 %all-reduce.10.cloned.1.call-done = f32[3,3,3,32,512]{3,2,1,0,4:T(4,128)} async-done(((f32[3,3,3,32,512]{3,2,1,0,4:T(4,128)}), f32[3,3,3,32,512]{3,2,1,0,4:T(4,128)}) %all-reduce.10.cloned.1.call-update) | async-done | bytes 1769488
  603.8 1.0 constant_dynamic-slice_fusion
  604.8 0.7 copy.56
  (7 shorter events, 0.0 us)
Async XLA Ops:
  8.0 17.3 %collective-permute-start.1 = (bf16[1,4,48,1,32]{2,4,3,1,0:T(8,128)(2,1)S(1)}, bf16[1,4,48,1,32]{2,4,3,1,0:T(8,128)(2,1)S(1)}, u32[]{:S(2)}, u32[]{:S(2)}) collective-permute-start(bf16[1,4,48,1,32]{2,4,3,1,0:T(8,128)(2,1)S(1)} %get-tuple-element.22), channel_id=1, source_target_pairs={{16,0},{32,16},{48,32},{64,48},{80,64},{96,80},{112,96},{128,112},... | collective-permute-start | bytes 36872 | tf_op jit(solution)/shard_map/ppermute | solution.py:17
  23.3 14.5 %collective-permute-start = (bf16[1,4,48,1,32]{2,4,3,1,0:T(8,128)(2,1)S(1)}, bf16[1,4,48,1,32]{2,4,3,1,0:T(8,128)(2,1)S(1)}, u32[]{:S(2)}, u32[]{:S(2)}) collective-permute-start(bf16[1,4,48,1,32]{2,4,3,1,0:T(8,128)(2,1)S(1)} %get-tuple-element.21), channel_id=1, source_target_pairs={{0,16},{16,32},{32,48},{48,64},{64,80},{80,96},{96,112},{112,128},... | collective-permute-start | bytes 36872 | tf_op jit(solution)/shard_map/ppermute | solution.py:15
  39.2 14.8 %copy-start.4 = (bf16[1,4,48,2,32]{2,4,3,1,0:T(8,128)(2,1)S(1)}, bf16[1,4,48,2,32]{2,4,3,1,0:T(8,128)(2,1)}, u32[]{:S(2)}) copy-start(bf16[1,4,48,2,32]{2,4,3,1,0:T(8,128)(2,1)} %param.3) | copy-start | bytes 73732
  43.1 42.0 %all-to-all-start = ((bf16[16,2,12288]{2,1,0:T(2,128)(2,1)}), bf16[16,2,12288]{2,1,0:T(2,128)(2,1)S(1)}, u32[]{:S(2)}, u32[]{:S(2)}) async-start(bf16[16,2,12288]{2,1,0:T(2,128)(2,1)} %reshape.428), calls=%async_computation | async-start | bytes 1572864 | tf_op jit(solution)/shard_map/all_to_all | solution.py:45
  53.7 550.0 %all-reduce.10.cloned.1.call-start = ((), (), s32[]{:S(2)}) async-start(), calls=%async_computation.1 | async-start | bytes 18874368
  95.9 4.7 copy-start
  100.5 1.0 copy-start.1
  100.5 1.4 copy-start.2
  118.1 4.7 copy-start.3
Sparse Core Ops, SparseCore 0:
  112.6 491.1 all-reduce.9
